TPU v7x, 512 devices: a whole 4x8x8 slice. The times are simulated.
512 devices in a mesh: inst: 16 (over z_lo, x, core), zone: 32 (over z_hi, y).
Axes of the slice: x: 4, y: 8, z: 8 (z_hi: 4, z_lo: 2; z = z_hi * 2 + z_lo), core: 2. Of those that a mesh axis runs over, the one named last changes fastest.
Arguments:
- state: float32 [16, 4096, 320], P('inst', 'zone'), may hold values from -6 to 6
- source: float32 [16, 4096, 320], P('inst', 'zone'), may hold values from -6 to 6
- jac_table: bfloat16 [256, 320, 320], P('zone'), may hold values from -0.3125 to 0.3125
- pattern_col: int32 [4096, 4], P('zone'), may hold values from 0 to 127
- pattern_type: int32 [4096, 4], P('zone'), may hold values from 0 to 7
- pseudo_step: float32 [16, 4096], P('inst', 'zone'), may hold values from 0.05 to 0.4
- zone_count: int32 [32], P('zone'), may hold values from 64 to 128, as said below
- link_src: int32 [16, 1024], P('inst', 'zone'), may hold values from 0 to 127
- link_owner: int32 [16, 1024, 1], P('inst', 'zone'), may hold values from 0 to 31; in each aligned block of 32 rows (0 to 31, 32 to 63, ..., all dimensions but the last counted through in order) at most 2 rows name the same one
- link_dest: int32 [16, 1024], P('inst', 'zone'), may hold values from 0 to 127
- link_weight: int32 [16, 1024], P('inst', 'zone'), may hold values from 0 to 15
- iface_table: float32 [16, 320], replicated, may hold values from 0.5 to 1.5
Outputs:
- updated: float32 [16, 4096, 320], P('inst', 'zone')
- residual: float32 [16, 4096, 320], P('inst', 'zone')
Inputs may be any that keep to these rules, and one draw needn't show every extreme that they name: `link_owner`: among the 32 links of one zone at one instance, no owner zone is named more than 2 times; in some of them one zone is named exactly 2 times. `zone_count`: some zone uses all 128 clusters.
All inputs are finite; a program needn't handle non-finite values.
Results may differ from a plain program's by a relative error of at most 0.0014.
Values sent between devices are 32-bit elements; how exact they have to be, the bound alone decides.
A program may use at most 64 MiB of HBM per device.

v0:
```python
import math

import jax
import jax.numpy as jnp
from jax import lax
from jax.sharding import PartitionSpec as P

OMEGA = 0.25
NU = 0.1


def coefficient(shift_steps, period):
    steps_f = shift_steps.astype(jnp.float32)
    parity = 1.0 - 2.0 * (shift_steps % 2).astype(jnp.float32)
    phase = math.pi * steps_f / period
    sine_safe = jnp.where(shift_steps == 0, 1.0, jnp.sin(phase))
    derive = OMEGA * parity * jnp.cos(phase) / sine_safe
    damping = NU * parity / (2.0 * sine_safe * sine_safe)
    centre = NU * (period * period + 2) / 12.0
    return jnp.where(shift_steps == 0, centre, derive + damping)


def on_device(
    state,
    source,
    jac_table,
    pattern_col,
    pattern_type,
    pseudo_step,
    zone_count,
    link_src,
    link_owner,
    link_dest,
    link_weight,
    iface_table,
):
    instances = lax.axis_size("inst")
    position = lax.axis_index("inst")
    zones = lax.axis_size("zone")
    local_state = state[0]
    clusters, width = local_state.shape
    kinds = jac_table.shape[0]
    state_half = local_state.astype(jnp.bfloat16)
    table_flat = jac_table.reshape(kinds * width, width)
    products = lax.dot_general(
        state_half, table_flat, (((1,), (1,)), ((), ())), preferred_element_type=jnp.float32
    )
    products = products.reshape(clusters * kinds, width)
    entry_rows = pattern_col * kinds + pattern_type
    jac_term = jnp.sum(products[entry_rows], axis=1)
    received = lax.all_gather(state, "inst", axis=0, tiled=True)
    senders = jnp.arange(received.shape[0], dtype=jnp.int32)
    weights = coefficient((position - senders) % instances, instances)
    time_term = jnp.einsum("m,mcw->cw", weights, received, precision=lax.Precision.HIGHEST)
    links = link_src.shape[1]
    slots_per = 2 * links // zones
    link_sources = link_src[0]
    link_owners = link_owner[0, :, 0]
    link_targets = link_dest[0]
    weight_sets = iface_table.shape[0]
    choose_sets = (
        link_weight[0][:, None] == jnp.arange(weight_sets, dtype=jnp.int32)[None, :]
    ).astype(jnp.float32)
    scales = jnp.dot(choose_sets, iface_table, precision=lax.Precision.HIGHEST)
    blocks = local_state[link_sources] * scales
    cluster_ids = jnp.arange(clusters, dtype=jnp.int32)
    owner_hits = (link_owners[:, None] == jnp.arange(zones, dtype=jnp.int32)[None, :]).astype(
        jnp.int32
    )
    order_rank = jnp.sum(jnp.cumsum(owner_hits, axis=0) * owner_hits, axis=1) - 1
    slot_ids = link_owners * slots_per + order_rank
    placing = (jnp.arange(zones * slots_per, dtype=jnp.int32)[:, None] == slot_ids[None, :]).astype(
        jnp.float32
    )
    outgoing = jnp.dot(placing, blocks, precision=lax.Precision.HIGHEST)
    outgoing_targets = jnp.sum(placing * link_targets.astype(jnp.float32)[None, :], axis=1)
    incoming, incoming_targets = (
        lax.all_to_all(outgoing, "zone", split_axis=0, concat_axis=0, tiled=True),
        lax.all_to_all(outgoing_targets, "zone", split_axis=0, concat_axis=0, tiled=True),
    )
    landing = (cluster_ids[:, None] == incoming_targets.astype(jnp.int32)[None, :]).astype(
        jnp.float32
    )
    iface = jnp.dot(landing, incoming, precision=lax.Precision.HIGHEST)
    active = cluster_ids < zone_count[0]
    residual = jnp.where(
        active[:, None], source[0] + jac_term + time_term - iface, jnp.float32(0.0)
    )
    updated = local_state - pseudo_step[0][:, None] * residual
    return (updated[None], residual[None])


def solution(mesh):
    placed = (
        P("inst", "zone", None),
        P("inst", "zone", None),
        P("zone", None, None),
        P("zone", None),
        P("zone", None),
        P("inst", "zone"),
        P("zone"),
        P("inst", "zone"),
        P("inst", "zone", None),
        P("inst", "zone"),
        P("inst", "zone"),
        P(),
    )
    return jax.shard_map(
        on_device,
        mesh=mesh,
        in_specs=placed,
        out_specs=(P("inst", "zone", None), P("inst", "zone", None)),
        check_vma=False,
    )
```

profile of v0, /device:TPU:6, one launch (start us, length us, event | category | flops | bytes accessed | tf_op | source)
XLA Modules:
  0.0 74.7 jit_solution(13736657775045834775)
XLA Ops:
  7.2 0.7 all-gather.2.cloned.1.call-update
  7.9 0.7 fusion.8
  8.6 0.1 reduce_window_sum.11
  8.7 0.8 %select_reduce_fusion.1 = s32[32]{0:T(128)S(1)} fusion(s32[32,32]{1,0:T(8,128)S(1)} %reduce_window_sum.11, s32[32]{0:T(128)} %bitcast.43), kind=kLoop, calls=%fused_computation.18 | loop fusion | flops 3040 | bytes 4352 | tf_op jit(solution)/shard_map/reduce_sum | solution.py:70
  9.5 0.7 convert_bitcast_fusion
  10.2 0.7 add_add_fusion
  10.9 0.1 select_reduce_fusion
  10.9 0.7 all_to_all.14
  11.7 16.0 %all-to-all-start = ((f32[32,2,1]{1,2,0:T(1,128)}), f32[32,2,1]{1,2,0:T(1,128)S(1)}, u32[]{:S(2)}, u32[]{:S(2)}) async-start(f32[32,2,1]{1,2,0:T(1,128)} %bitcast.10), calls=%async_computation | async-start | bytes 32768 | tf_op jit(solution)/shard_map/all_to_all | solution.py:79
  27.6 1.0 %copy.24 = f32[128,320]{1,0:T(8,128)S(1)} copy(f32[128,320]{0,1:T(8,128)} %bitcast.39) | data formatting | bytes 327680 | tf_op jit(solution)/shard_map/squeeze | solution.py:40
  28.7 0.7 compare_select_fusion
  29.4 0.1 copy.21
  29.5 0.1 reshape.69
  29.6 0.7 fusion.21
  30.3 0.6 gather_fusion.1
  30.9 1.0 %convolution_multiply_fusion = f32[32,320]{1,0:T(8,128)S(1)} fusion(f32[32,320]{1,0:T(8,128)S(1)} %gather_fusion.1, f32[16,320]{1,0:T(8,128)} %param.23, s32[32]{0:T(128)} %bitcast.44), kind=kOutput, calls=%fused_computation.6 | convolution fusion | flops 1976832 | bytes 102528 | tf_op jit(solution)/shard_map/dot_general | solution.py:64
  31.9 0.3 fusion.9
  32.2 2.8 %fusion.4 = f32[128,2560]{1,0:T(8,128)} fusion(bf16[2560,320]{1,0:T(8,128)(2,1)S(1)} %bitcast.38, f32[1,128,320]{1,2,0:T(8,128)} %param.12), kind=kOutput, calls=%fused_computation.10 | convolution fusion | flops 209756160 | bytes 3112960 | tf_op jit(solution)/shard_map/dot_general | solution.py:45
  35.0 0.7 all_to_all.16
  36.3 3.5 %all-to-all-done = f32[32,2,1]{1,2,0:T(1,128)S(1)} async-done(((f32[32,2,1]{1,2,0:T(1,128)}), f32[32,2,1]{1,2,0:T(1,128)S(1)}, u32[]{:S(2)}, u32[]{:S(2)}) %all-to-all-start) | async-done | bytes 288 | tf_op jit(solution)/shard_map/all_to_all | solution.py:79
  39.9 8.8 %all-to-all-start.1 = ((f32[32,2,320]{2,1,0:T(2,128)}), f32[32,2,320]{2,1,0:T(2,128)}, u32[]{:S(2)}, u32[]{:S(2)}) async-start(f32[32,2,320]{2,1,0:T(2,128)} %all_to_all.16), calls=%async_computation.1 | async-start | bytes 196608 | tf_op jit(solution)/shard_map/all_to_all | solution.py:78
  48.7 1.7 %reshape.66 = f32[1024,320]{1,0:T(8,128)S(1)} reshape(f32[128,2560]{1,0:T(8,128)} %fusion.4) | data formatting | bytes 2621440 | tf_op jit(solution)/shard_map/reshape | solution.py:48
  50.4 2.3 %gather_fusion = f32[512,320]{1,0:T(8,128)} fusion(f32[1024,320]{1,0:T(8,128)S(1)} %reshape.66, s32[1024]{0:T(1024)S(1)} %pad_clamp_fusion.1), kind=kCustom, calls=%fused_computation | custom fusion | bytes 1312768 | tf_op jit(solution)/shard_map/gather | solution.py:50
  52.8 1.4 %reshape.72 = f32[128,4,320]{2,1,0:T(4,128)S(1)} reshape(f32[512,320]{1,0:T(8,128)} %gather_fusion) | data formatting | bytes 1310720 | tf_op jit(solution)/shard_map/gather | solution.py:50
  54.1 0.5 reduce_sum.27
  54.6 0.1 copy.22
  54.8 0.1 convert_element_type.39
  54.9 6.4 %all-to-all-done.1 = f32[32,2,320]{2,1,0:T(2,128)} async-done(((f32[32,2,320]{2,1,0:T(2,128)}), f32[32,2,320]{2,1,0:T(2,128)}, u32[]{:S(2)}, u32[]{:S(2)}) %all-to-all-start.1) | async-done | bytes 81952 | tf_op jit(solution)/shard_map/all_to_all | solution.py:78
  61.3 1.0 %all_to_all.18 = f32[64,320]{1,0:T(8,128)S(1)} reshape(f32[32,2,320]{2,1,0:T(2,128)} %all-to-all-done.1) | data formatting | bytes 163840 | tf_op jit(solution)/shard_map/all_to_all | solution.py:78
  62.3 4.5 %fusion = f32[1,128,320]{1,0,2:T(1,128)S(1)} fusion(f32[16,128,320]{1,2,0:T(8,128)} %all-gather.2.cloned.1.call-done, s32[]{:T(128)S(6)} %axis_index.15), kind=kOutput, calls=%fused_computation.2 | convolution fusion | flops 7864944 | bytes 2785284 | tf_op jit(solution)/shard_map/m,mcw->cw/dot_general | solution.py:54
  66.8 0.3 fusion.2
  67.2 0.7 subtract_bitcast_fusion
  (20 shorter events, 0.2 us)
Async XLA Ops:
  7.2 25.0 %copy-start = (bf16[8,320,320]{2,1,0:T(8,128)(2,1)S(1)}, bf16[8,320,320]{2,1,0:T(8,128)(2,1)}, u32[]{:S(2)}) copy-start(bf16[8,320,320]{2,1,0:T(8,128)(2,1)} %param.14) | copy-start | bytes 4915204
  7.2 55.1 %all-gather.2.cloned.1.call-start = ((), (), s32[]{:S(2)}) async-start(), calls=%async_computation.2 | async-start | bytes 2785280 | tf_op jit(solution)/shard_map/all_gather | solution.py:51
  11.7 28.2 %all-to-all-start = ((f32[32,2,1]{1,2,0:T(1,128)}), f32[32,2,1]{1,2,0:T(1,128)S(1)}, u32[]{:S(2)}, u32[]{:S(2)}) async-start(f32[32,2,1]{1,2,0:T(1,128)} %bitcast.10), calls=%async_computation | async-start | bytes 32768 | tf_op jit(solution)/shard_map/all_to_all | solution.py:79
  39.9 8.8 %copy-start.4 = (f32[32,2,1]{1,2,0:T(1,128)}, f32[32,2,1]{1,2,0:T(1,128)S(1)}, u32[]{:S(2)}) copy-start(f32[32,2,1]{1,2,0:T(1,128)S(1)} %all-to-all-done) | copy-start | bytes 772
  39.9 21.5 %all-to-all-start.1 = ((f32[32,2,320]{2,1,0:T(2,128)}), f32[32,2,320]{2,1,0:T(2,128)}, u32[]{:S(2)}, u32[]{:S(2)}) async-start(f32[32,2,320]{2,1,0:T(2,128)} %all_to_all.16), calls=%async_computation.1 | async-start | bytes 196608 | tf_op jit(solution)/shard_map/all_to_all | solution.py:78
  52.8 2.0 %copy-start.5 = (f32[32,2,1]{1,2,0:T(1,128)S(1)}, f32[32,2,1]{1,2,0:T(1,128)}, u32[]{:S(2)}) copy-start(f32[32,2,1]{1,2,0:T(1,128)} %copy-done.4) | copy-start | bytes 772
  54.1 12.6 %copy-start.3 = (f32[1,128,320]{1,2,0:T(8,128)S(1)}, f32[1,128,320]{1,2,0:T(8,128)}, u32[]{:S(2)}) copy-start(f32[1,128,320]{1,2,0:T(8,128)} %param.13) | copy-start | bytes 491524
  54.7 12.4 %copy-start.1 = (f32[1,128,320]{1,2,0:T(8,128)S(1)}, f32[1,128,320]{1,2,0:T(8,128)}, u32[]{:S(2)}) copy-start(f32[1,128,320]{1,2,0:T(8,128)} %param.12) | copy-start | bytes 491524
  54.7 12.4 %copy-start.6 = (f32[1,128]{1,0:T(1,128)S(1)}, f32[1,128]{1,0:T(1,128)}, u32[]{:S(2)}) copy-start(f32[1,128]{1,0:T(1,128)} %param.17) | copy-start | bytes 1540
  67.1 0.8 %copy-start.2 = (f32[128,320]{0,1:T(8,128)}, f32[128,320]{0,1:T(8,128)S(1)}, u32[]{:S(2)}) copy-start(f32[128,320]{0,1:T(8,128)S(1)} %fusion.2) | copy-start | bytes 491524
Sparse Core Ops, SparseCore 0:
  10.1 43.8 all-gather.1
where the time goes:
time: 75.2 us; the launch traced here: 74.7 us
  starting transfers between devices  24.8 us (33%)
  between operations  14.9 us (20%)
  waiting for transfers between devices  10.6 us (14%)
  local copies, waits for them, and re-layouts  9.92 us (13%)
  matrix products  8.83 us (12%)
  other arithmetic  5.7 us (8%)
    all_to_all x1, starting transfers between devices, on_device(): lax.all_to_all(outgoing_targets, 'zone', split_axis=0, concat_axis=0, til...  16 us
    all_to_all x1, starting transfers between devices, on_device(): lax.all_to_all(outgoing, 'zone', split_axis=0, concat_axis=0, tiled=True)  8.79 us
    all_to_all x1, waiting for transfers between devices, on_device(): lax.all_to_all(outgoing, 'zone', split_axis=0, concat_axis=0, tiled=True)  6.38 us
    dot_general x1, matrix products, on_device(): jnp.einsum('m,mcw->cw', weights, received, precision=lax.Precision.HIGHEST)  4.45 us
    gather x2, local copies, waits for them, and re-layouts, on_device(): jac_term = jnp.sum(products[entry_rows], axis=1)  3.69 us
    all_to_all x1, waiting for transfers between devices, on_device(): lax.all_to_all(outgoing_targets, 'zone', split_axis=0, concat_axis=0, til...  3.53 us
    dot_general x1, matrix products, on_device(): lax.dot_general(state_half, table_flat, (((1,), (1,)), ((), ())), preferr...  2.77 us
    reshape x1, local copies, waits for them, and re-layouts, on_device(): products = products.reshape(clusters * kinds, width)  1.74 us
  transfers between devices with their start and end apart: 3, of which 2 were waited for; matrix products, arithmetic and copies ran while one was open for 22% of the time, Pallas kernels for 0%

commit v1 on v0

v1 whole, which is shorter than its diff:
```python
import math

import jax
import jax.numpy as jnp
from jax import lax
from jax.experimental import pallas as pl
from jax.experimental.pallas import tpu as pltpu
from jax.sharding import PartitionSpec as P

OMEGA = 0.25
NU = 0.1
MESH = pl.DeviceIdType.MESH

NZ, NX, NC = 2, 4, 2
NH, NY = 4, 8
NT = NZ * NX * NC
ROWS = (24, 16)
CHIP_ROWS = 40
OFFSETS = tuple(
    (dz, dx, dc)
    for dz, dx in ((1, 2), (0, 2), (1, 1), (1, 3), (0, 1), (0, 3), (1, 0), (0, 0))
    for dc in (0, 1)
    if (dz, dx, dc) != (0, 0, 0)
)
Y_STEPS = (4, 3, 5, 2, 6, 1, 7)
H_STEPS = (2, 1, 3)


def coefficients():
    values = []
    for k in range(NT):
        if k == 0:
            values.append(NU * (NT * NT + 2) / 12.0)
            continue
        phase = math.pi * k / NT
        sign = -1.0 if k % 2 else 1.0
        values.append(
            OMEGA * sign * math.cos(phase) / math.sin(phase)
            + NU * sign / (2.0 * math.sin(phase) ** 2)
        )
    return values


def split(value):
    high = value.astype(jnp.bfloat16)
    low = (value - high.astype(jnp.float32)).astype(jnp.bfloat16)
    return high, low


def dot(a, b, a_axis, b_axis):
    return lax.dot_general(
        a, b, (((a_axis,), (b_axis,)), ((), ())), preferred_element_type=jnp.float32
    )


def kernel(
    state_hbm,
    source_hbm,
    jac_hbm,
    col_hbm,
    type_hbm,
    src_hbm,
    owner_hbm,
    dest_hbm,
    weight_hbm,
    table_hbm,
    out_ref,
    state,
    source,
    jac,
    col,
    kind,
    link_src,
    link_owner,
    link_dest,
    link_weight,
    table,
    spread_in,
    spread_out,
    time_term,
    y_out,
    y_in,
    h_out,
    h_in,
    local_sem,
    send1,
    recv1,
    send2,
    recv2,
    send_y,
    recv_y,
    send_h,
    recv_h,
):
    me = lax.axis_index("inst")
    zone = lax.axis_index("zone")
    z, x, core = me // (NX * NC), (me // NC) % NX, me % NC
    h, y = zone // NY, zone % NY

    def instance(dz, dx, core_there):
        return ((z + dz) % NZ) * (NX * NC) + ((x + dx) % NX) * NC + core_there

    barrier = pltpu.get_barrier_semaphore()

    def greet(inst_there, zone_there):
        pl.semaphore_signal(
            barrier, inc=1, device_id=(inst_there, zone_there), device_id_type=MESH
        )

    for dy in Y_STEPS:
        greet(me, h * NY + (y + dy) % NY)
    for dh in H_STEPS:
        greet(me, ((h + dh) % NH) * NY + y)
    for dz, dx, dc in OFFSETS:
        greet(instance(dz, dx, (core + dc) % NC), zone)

    pairs = (
        (owner_hbm, link_owner),
        (src_hbm, link_src),
        (dest_hbm, link_dest),
        (weight_hbm, link_weight),
        (table_hbm, table),
        (state_hbm, state),
        (col_hbm, col),
        (type_hbm, kind),
        (jac_hbm, jac),
        (source_hbm, source),
    )
    loads = [
        pltpu.make_async_copy(a, b, local_sem.at[i]) for i, (a, b) in enumerate(pairs)
    ]
    for load in loads:
        load.start()
    for load in loads[:6]:
        load.wait()

    links = link_owner.shape[1]
    owner_row = link_owner[...]
    lane = lax.broadcasted_iota(jnp.int32, (links, links), 1)
    sub = lax.broadcasted_iota(jnp.int32, (links, links), 0)
    owner_grid = jnp.broadcast_to(owner_row, (links, links)).astype(jnp.float32)
    owner_col = jnp.sum(jnp.where(lane == sub, owner_grid, 0.0), axis=1, keepdims=True)
    earlier = (owner_col == owner_grid) & (sub < lane)
    rank_row = jnp.sum(jnp.where(earlier, 1.0, 0.0), axis=0, keepdims=True).astype(jnp.int32)
    slot_row = (owner_row & (NY - 1)) * (2 * NH) + (owner_row >> 3) * 2 + rank_row
    code_row = (
        1 + link_src[...] + 128 * link_dest[...] + 16384 * link_weight[...]
    ).astype(jnp.float32)
    slots = 2 * NH * NY
    slot_ids = lax.broadcasted_iota(jnp.int32, (slots, links), 0)
    code_col = jnp.sum(
        jnp.where(
            slot_ids == jnp.broadcast_to(slot_row, (slots, links)),
            jnp.broadcast_to(code_row, (slots, links)),
            0.0,
        ),
        axis=1,
        keepdims=True,
    ).astype(jnp.int32)
    used = code_col > 0
    bare = code_col - 1
    src_col = bare & 127
    target_col = jnp.where(used, ((bare >> 7) & 127) + 1, 0).astype(jnp.float32)
    weight_col = jnp.where(used, bare >> 14, -1)
    pick_src = jnp.where(
        jnp.broadcast_to(src_col, (slots, 128))
        == lax.broadcasted_iota(jnp.int32, (slots, 128), 1),
        1.0,
        0.0,
    ).astype(jnp.bfloat16)
    sets = table.shape[0]
    pick_set = jnp.where(
        jnp.broadcast_to(weight_col, (slots, sets))
        == lax.broadcasted_iota(jnp.int32, (slots, sets), 1),
        1.0,
        0.0,
    ).astype(jnp.bfloat16)
    state_high, state_low = split(state[...])
    table_high, table_low = split(table[...])
    blocks = dot(pick_src, state_high, 1, 1) + dot(pick_src, state_low, 1, 1)
    scales = dot(pick_set, table_high, 1, 0) + dot(pick_set, table_low, 1, 0)
    sending = blocks * scales
    y_out[0] = sending[:, 0:128]
    y_out[1] = sending[:, 128:256]
    y_out[2, :, 0:64] = sending[:, 256:320]
    y_out[2, :, 64:128] = jnp.broadcast_to(target_col, (slots, 64))

    pl.semaphore_wait(barrier, len(Y_STEPS) + len(H_STEPS) + len(OFFSETS))

    def first_copy(i, here):
        dz, dx, dc = OFFSETS[i]
        there = (here + dc) % NC
        base = CHIP_ROWS * (((z + dz) % NZ) * NX + (x + dx) % NX) + ROWS[0] * there
        return pltpu.make_async_remote_copy(
            src_ref=state.at[pl.ds(pl.multiple_of(base, 8), ROWS[there])],
            dst_ref=spread_in.at[me, pl.ds(0, ROWS[there])],
            send_sem=send1.at[i],
            recv_sem=recv1.at[i],
            device_id=(instance(dz, dx, there), zone),
            device_id_type=MESH,
        )

    def first_arrival(i, here):
        dz, dx, dc = OFFSETS[i]
        there = (here + dc) % NC
        sender = instance(NZ - dz, NX - dx, there)
        landed = spread_in.at[sender, pl.ds(0, ROWS[here])]
        return pltpu.make_async_remote_copy(
            src_ref=landed,
            dst_ref=landed,
            send_sem=send1.at[i],
            recv_sem=recv1.at[i],
            device_id=(sender, zone),
            device_id_type=MESH,
        )

    def my_base(here):
        return pl.multiple_of(CHIP_ROWS * (z * NX + x) + ROWS[0] * here, 8)

    def second_copy(i, here):
        dz, dx, dc = OFFSETS[i]
        there = (here + dc) % NC
        target = instance(dz, dx, there)
        return pltpu.make_async_remote_copy(
            src_ref=spread_out.at[target, pl.ds(0, ROWS[here])],
            dst_ref=time_term.at[pl.ds(my_base(here), ROWS[here])],
            send_sem=send2.at[i],
            recv_sem=recv2.at[i],
            device_id=(target, zone),
            device_id_type=MESH,
        )

    def second_arrival(i, here):
        dz, dx, dc = OFFSETS[i]
        there = (here + dc) % NC
        base = (
            CHIP_ROWS * (((z + NZ - dz) % NZ) * NX + (x + NX - dx) % NX) + ROWS[0] * there
        )
        landed = time_term.at[pl.ds(pl.multiple_of(base, 8), ROWS[there])]
        return pltpu.make_async_remote_copy(
            src_ref=landed,
            dst_ref=landed,
            send_sem=send2.at[i],
            recv_sem=recv2.at[i],
            device_id=(instance(NZ - dz, NX - dx, there), zone),
            device_id_type=MESH,
        )

    def y_copy(i):
        there = (y + Y_STEPS[i]) % NY
        return pltpu.make_async_remote_copy(
            src_ref=y_out.at[:, pl.ds(pl.multiple_of(there * 8, 8), 8)],
            dst_ref=y_in.at[:, pl.ds(pl.multiple_of(y * 8, 8), 8)],
            send_sem=send_y.at[i],
            recv_sem=recv_y.at[i],
            device_id=(me, h * NY + there),
            device_id_type=MESH,
        )

    def y_arrival(i):
        sender = (y + NY - Y_STEPS[i]) % NY
        landed = y_in.at[:, pl.ds(pl.multiple_of(sender * 8, 8), 8)]
        return pltpu.make_async_remote_copy(
            src_ref=landed,
            dst_ref=landed,
            send_sem=send_y.at[i],
            recv_sem=recv_y.at[i],
            device_id=(me, h * NY + sender),
            device_id_type=MESH,
        )

    def h_copy(i):
        there = (h + H_STEPS[i]) % NH
        return pltpu.make_async_remote_copy(
            src_ref=h_out.at[there],
            dst_ref=h_in.at[h],
            send_sem=send_h.at[i],
            recv_sem=recv_h.at[i],
            device_id=(me, there * NY + y),
            device_id_type=MESH,
        )

    def h_arrival(i):
        sender = (h + NH - H_STEPS[i]) % NH
        return pltpu.make_async_remote_copy(
            src_ref=h_in.at[sender],
            dst_ref=h_in.at[sender],
            send_sem=send_h.at[i],
            recv_sem=recv_h.at[i],
            device_id=(me, sender * NY + y),
            device_id_type=MESH,
        )

    def on_core(step):
        for here in range(NC):

            @pl.when(core == here)
            def _():
                step(here)

    def start_first(here):
        for i in range(len(OFFSETS)):
            first_copy(i, here).start()

    on_core(start_first)
    for i in range(len(Y_STEPS)):
        y_copy(i).start()

    def keep_own(here):
        spread_in[me, 0 : ROWS[here]] = state[pl.ds(my_base(here), ROWS[here])]

    on_core(keep_own)
    own_rows = pl.ds(pl.multiple_of(y * 8, 8), 8)
    y_in[:, own_rows] = y_out[:, own_rows]

    for load in loads[6:]:
        load.wait()
    clusters = state.shape[1]
    key = kind[...] * clusters + col[...]
    cluster_ids = lax.broadcasted_iota(jnp.int32, (clusters, clusters), 0)
    total = None
    for t in range(jac.shape[0]):
        hits = None
        for j in range(key.shape[0]):
            row = jnp.broadcast_to(key[j : j + 1] - t * clusters, (clusters, clusters))
            hit = jnp.where(cluster_ids == row, 1.0, 0.0)
            hits = hit if hits is None else hits + hit
        gathered = dot(state_high, hits.astype(jnp.bfloat16), 1, 0)
        gathered_high, gathered_low = split(gathered)
        both = jnp.concatenate([gathered_high, gathered_low], axis=1)
        product = dot(jac[t], both, 1, 0)
        total = product if total is None else total + product
    out_ref[...] = source[...] + (total[:, 0:clusters] + total[:, clusters:])

    coeff = coefficients()

    def transform(here):
        for i in range(len(OFFSETS)):
            first_arrival(i, here).wait_recv()
        for r in range(0, ROWS[here], 8):
            parts = [spread_in[m, r : r + 8] for m in range(NT)]
            for n in range(NT):
                value = parts[0] * coeff[n]
                for m in range(1, NT):
                    value = value + parts[m] * coeff[(n - m) % NT]
                spread_out[n, r : r + 8] = value
        for i in range(len(OFFSETS)):
            second_copy(i, here).start()
        time_term[pl.ds(my_base(here), ROWS[here])] = spread_out[me, 0 : ROWS[here]]

    on_core(transform)

    for i in range(len(Y_STEPS)):
        y_arrival(i).wait_recv()
    for there in range(NH):
        for rank in range(2):
            for c in range(3):
                h_out[there, c, rank * 8 : rank * 8 + 8] = y_in[
                    c, pl.ds(there * 2 + rank, 8, stride=8)
                ]
    for i in range(len(H_STEPS)):
        h_copy(i).start()
    h_in[h] = h_out[h]
    for i in range(len(H_STEPS)):
        h_arrival(i).wait_recv()

    tail = h_in[:, 2].reshape(slots, 128)
    lanes = lax.broadcasted_iota(jnp.int32, (slots, 128), 1)
    targets = jnp.where(lanes < 64, pltpu.roll(tail, 64, 1), tail)
    landing = jnp.where(targets == (lanes + 1).astype(jnp.float32), 1.0, 0.0).astype(
        jnp.bfloat16
    )
    for c, rows in enumerate((128, 128, 64)):
        chunk = tail if c == 2 else h_in[:, c].reshape(slots, 128)
        high, low = split(chunk)
        iface = dot(high, landing, 0, 0) + dot(low, landing, 0, 0)
        at = pl.ds(c * 128, rows)
        out_ref[at] = out_ref[at] - iface[0:rows]

    def finish(here):
        for i in range(len(OFFSETS)):
            second_arrival(i, here).wait_recv()

    on_core(finish)
    out_ref[...] = out_ref[...] + time_term[...]

    def drain(here):
        for i in range(len(OFFSETS)):
            first_copy(i, here).wait_send()
            second_copy(i, here).wait_send()

    on_core(drain)
    for i in range(len(Y_STEPS)):
        y_copy(i).wait_send()
    for i in range(len(H_STEPS)):
        h_copy(i).wait_send()


def on_device(
    state,
    source,
    jac_table,
    pattern_col,
    pattern_type,
    pseudo_step,
    zone_count,
    link_src,
    link_owner,
    link_dest,
    link_weight,
    iface_table,
):
    state_t = state[0].T
    source_t = source[0].T
    width, clusters = state_t.shape
    kinds = jac_table.shape[0]
    links = link_src.shape[1]
    f32, i32, bf16 = jnp.float32, jnp.int32, jnp.bfloat16
    dma = pltpu.SemaphoreType.DMA
    combined = pl.pallas_call(
        kernel,
        out_shape=jax.ShapeDtypeStruct((width, clusters), f32),
        in_specs=[pl.BlockSpec(memory_space=pl.ANY)] * 10,
        out_specs=pl.BlockSpec(memory_space=pltpu.VMEM),
        scratch_shapes=[
            pltpu.VMEM((width, clusters), f32),
            pltpu.VMEM((width, clusters), f32),
            pltpu.VMEM((kinds, width, width), bf16),
            pltpu.VMEM((4, clusters), i32),
            pltpu.VMEM((4, clusters), i32),
            pltpu.VMEM((1, links), i32),
            pltpu.VMEM((1, links), i32),
            pltpu.VMEM((1, links), i32),
            pltpu.VMEM((1, links), i32),
            pltpu.VMEM(iface_table.shape, f32),
            pltpu.VMEM((NT, ROWS[0], clusters), f32),
            pltpu.VMEM((NT, ROWS[0], clusters), f32),
            pltpu.VMEM((width, clusters), f32),
            pltpu.VMEM((3, 2 * NH * NY, 128), f32),
            pltpu.VMEM((3, 2 * NH * NY, 128), f32),
            pltpu.VMEM((NH, 3, 2 * NY, 128), f32),
            pltpu.VMEM((NH, 3, 2 * NY, 128), f32),
            dma((10,)),
            dma((len(OFFSETS),)),
            dma((len(OFFSETS),)),
            dma((len(OFFSETS),)),
            dma((len(OFFSETS),)),
            dma((len(Y_STEPS),)),
            dma((len(Y_STEPS),)),
            dma((len(H_STEPS),)),
            dma((len(H_STEPS),)),
        ],
        compiler_params=pltpu.CompilerParams(collective_id=0, has_side_effects=True),
        name="section",
    )(
        state_t,
        source_t,
        jac_table,
        pattern_col.T,
        pattern_type.T,
        link_src,
        link_owner.reshape(1, links),
        link_dest,
        link_weight,
        iface_table,
    )
    active = jnp.arange(clusters, dtype=jnp.int32) < zone_count[0]
    residual = jnp.where(active[None, :], combined, jnp.float32(0.0))
    updated = state_t - pseudo_step * residual
    return (updated.T[None], residual.T[None])


def solution(mesh):
    placed = (
        P("inst", "zone", None),
        P("inst", "zone", None),
        P("zone", None, None),
        P("zone", None),
        P("zone", None),
        P("inst", "zone"),
        P("zone"),
        P("inst", "zone"),
        P("inst", "zone", None),
        P("inst", "zone"),
        P("inst", "zone"),
        P(),
    )
    return jax.shard_map(
        on_device,
        mesh=mesh,
        in_specs=placed,
        out_specs=(P("inst", "zone", None), P("inst", "zone", None)),
        check_vma=False,
    )
```

time: 75.2 us -> 30.8 us (0.41)
  the two profiles are of different devices: /device:TPU:6 before, /device:TPU:1 now
where the time goes in v1:
time: 30.8 us; the launch traced here: 30.6 us
  Pallas kernels  27.6 us (90%)
  other arithmetic  1.67 us (5%)
  between operations  1.36 us (4%)
    pallas_call x1, Pallas kernels, on_device(): pl.pallas_call(kernel, out_shape=jax.ShapeDtypeStruct((width, clusters),...  27.6 us
    broadcast_in_dim x1, other arithmetic, on_device(): return (updated.T[None], residual.T[None])  1.66 us

profile of v1, /device:TPU:1, one launch (start us, length us, event | category | flops | bytes accessed | tf_op | source)
XLA Modules:
  0.0 30.6 jit_solution(2741789864822418531)
XLA Ops:
  0.6 0.0 copy-start
  0.6 0.0 copy-start.1
  1.3 27.6 %section.1 = f32[320,128]{1,0:T(8,128)} custom-call(f32[320,128]{1,0:T(8,128)} %bitcast.21, f32[320,128]{1,0:T(8,128)} %bitcast.22, bf16[8,320,320]{2,1,0:T(8,128)(2,1)} %jac_hbm.1, s32[4,128]{1,0:T(4,128)} %bitcast.23, s32[4,128]{1,0:T(4,128)} %bitcast.24, s32[1,32]{1,0:T(1,128)} %src_hbm.1, s32[1,32]{1,0:T(1,128)} %bitcast.26, s32[1,32]{1,0:T(1,128)} %dest_hbm.1, ...), custom_call_target="tpu_custom_call" | custom-call | tf_op jit(solution)/shard_map/section/pallas_call | solution.py:420
  28.9 0.0 copy-done
  28.9 0.0 copy-done.1
  28.9 1.7 %select_bitcast_fusion = (f32[1,128,320]{1,2,0:T(8,128)}, f32[1,128,320]{1,2,0:T(8,128)}) fusion(f32[320,128]{1,0:T(8,128)} %section.1, pred[128]{0:T(512)(128)(4,1)S(1)} %iota_compare_fusion, f32[128]{0:T(128)S(1)} %bitcast.25, f32[1,128,320]{1,2,0:T(8,128)S(1)} %copy-done), kind=kLoop, calls=%fused_computation.1 | loop fusion | flops 122880 | bytes 656000 | tf_op jit(solution)/shard_map/broadcast_in_dim | solution.py:470
  (1 shorter events, 0.0 us)
Async XLA Ops:
  0.6 28.3 %copy-start = (f32[1,128,320]{1,2,0:T(8,128)S(1)}, f32[1,128,320]{1,2,0:T(8,128)}, u32[]{:S(2)}) copy-start(f32[1,128,320]{1,2,0:T(8,128)} %param.12) | copy-start | bytes 491524
  0.6 28.3 %copy-start.1 = (f32[1,128]{1,0:T(1,128)S(1)}, f32[1,128]{1,0:T(1,128)}, u32[]{:S(2)}) copy-start(f32[1,128]{1,0:T(1,128)} %param.17) | copy-start | bytes 1540

commit v2 on v1

v2 whole, which is shorter than its diff:
```python
import math

import jax
import jax.numpy as jnp
from jax import lax
from jax.experimental import pallas as pl
from jax.experimental.pallas import tpu as pltpu
from jax.sharding import PartitionSpec as P

OMEGA = 0.25
NU = 0.1
MESH = pl.DeviceIdType.MESH

NZ, NX, NC = 2, 4, 2
NH, NY = 4, 8
NT = NZ * NX * NC
ROWS = (24, 16)
CHIP_ROWS = 40
CHIPS = NZ * NX
ZONES = NH * NY
BLOCK = 6


def y_place(y):
    return y + lax.div(y, 4) * (11 - 2 * y)


def coefficients():
    values = []
    for k in range(NT):
        if k == 0:
            values.append(NU * (NT * NT + 2) / 12.0)
            continue
        phase = math.pi * k / NT
        sign = -1.0 if k % 2 else 1.0
        values.append(
            OMEGA * sign * math.cos(phase) / math.sin(phase)
            + NU * sign / (2.0 * math.sin(phase) ** 2)
        )
    return values


def split(value):
    high = value.astype(jnp.bfloat16)
    low = (value - high.astype(jnp.float32)).astype(jnp.bfloat16)
    return high, low


def dot(a, b, a_axis, b_axis):
    return lax.dot_general(
        a, b, (((a_axis,), (b_axis,)), ((), ())), preferred_element_type=jnp.float32
    )


def each(low, high, step):
    def body(i, carry):
        step(i)
        return carry

    lax.fori_loop(low, high, body, 0)


def kernel(
    state_hbm,
    source_hbm,
    jac_hbm,
    col_hbm,
    type_hbm,
    src_hbm,
    owner_hbm,
    dest_hbm,
    weight_hbm,
    table_hbm,
    count_hbm,
    combined_ref,
    mask_ref,
    state,
    source,
    jac,
    col,
    kind,
    link_src,
    link_owner,
    link_dest,
    link_weight,
    table,
    count,
    total_ref,
    spread_in,
    spread_out,
    time_term,
    zone_out,
    zone_in,
    local_sem,
    send1,
    recv1,
    send2,
    recv2,
    send3,
    recv3,
    inst_ready,
    zone_ready,
):
    me = lax.axis_index("inst")
    zone = lax.axis_index("zone")
    chip, core = lax.div(me, NC), lax.rem(me, NC)
    h, y = lax.div(zone, NY), lax.rem(zone, NY)
    inst_shift = 1 - jnp.minimum(zone, 1)
    inst_mine = lax.rem(me + NT - inst_shift, NT)
    place = y_place(y)

    def inst_at(p):
        return lax.rem(p + inst_shift, NT)

    def zone_at(row, p):
        return row * NY + y_place(p)

    def far(low, high):
        return jnp.minimum(low + NH - 1 - high, 1)

    def reach(row, high):
        return NY - far(row, high) * (NY - 1 - place)

    def before(step):
        each(0, h, lambda row: each(0, reach(row, h), lambda p: step(row, p)))
        each(0, place, lambda p: step(h, p))

    def after(step):
        each(place + 1, NY, lambda p: step(h, p))
        each(h + 1, NH, lambda row: each(place * far(h, row), NY, lambda p: step(row, p)))

    barrier = pltpu.get_barrier_semaphore()

    def signal(sem, inst_there, zone_there):
        pl.semaphore_signal(
            sem, inc=1, device_id=(inst_there, zone_there), device_id_type=MESH
        )

    def wait_for(sem, number):
        @pl.when(number > 0)
        def _():
            pl.semaphore_wait(sem, number)

    pairs = (
        (owner_hbm, link_owner),
        (src_hbm, link_src),
        (dest_hbm, link_dest),
        (weight_hbm, link_weight),
        (table_hbm, table),
        (state_hbm, state),
        (col_hbm, col),
        (type_hbm, kind),
        (jac_hbm, jac),
        (source_hbm, source),
        (count_hbm, count),
    )
    loads = [
        pltpu.make_async_copy(a, b, local_sem.at[i]) for i, (a, b) in enumerate(pairs)
    ]
    for load in loads:
        load.start()

    each(inst_mine + 1, NT, lambda p: signal(barrier, inst_at(p), zone))
    after(lambda row, p: signal(barrier, me, zone_at(row, p)))

    last = lax.div(h, NH - 1)
    wait_for(barrier, inst_mine + (place + 1) * (h + 1) - 1 + last * (NY - 1 - place))
    each(0, inst_mine, lambda p: signal(inst_ready, inst_at(p), zone))
    before(lambda row, p: signal(zone_ready.at[h], me, zone_at(row, p)))

    for load in loads[:6]:
        load.wait()

    links = link_owner.shape[1]
    owner_row = link_owner[...]
    lane = lax.broadcasted_iota(jnp.int32, (links, links), 1)
    sub = lax.broadcasted_iota(jnp.int32, (links, links), 0)
    owner_grid = jnp.broadcast_to(owner_row, (links, links)).astype(jnp.float32)
    owner_col = jnp.sum(jnp.where(lane == sub, owner_grid, 0.0), axis=1, keepdims=True)
    earlier = (owner_col == owner_grid) & (sub < lane)
    order_row = jnp.sum(jnp.where(earlier, 1.0, 0.0), axis=0, keepdims=True).astype(
        jnp.int32
    )
    owner_y = owner_row & (NY - 1)
    slot_row = (
        order_row * ZONES + owner_row - owner_y + jnp.where(owner_y < 4, owner_y, 11 - owner_y)
    )
    code_row = (
        1 + link_src[...] + 128 * link_dest[...] + 16384 * link_weight[...]
    ).astype(jnp.float32)
    slots = 2 * ZONES
    slot_ids = lax.broadcasted_iota(jnp.int32, (slots, links), 0)
    code_col = jnp.sum(
        jnp.where(
            slot_ids == jnp.broadcast_to(slot_row, (slots, links)),
            jnp.broadcast_to(code_row, (slots, links)),
            0.0,
        ),
        axis=1,
        keepdims=True,
    ).astype(jnp.int32)
    used = code_col > 0
    bare = code_col - 1
    src_col = bare & 127
    target_col = jnp.where(used, ((bare >> 7) & 127) + 1, 0).astype(jnp.float32)
    weight_col = jnp.where(used, bare >> 14, -1)
    pick_src = jnp.where(
        jnp.broadcast_to(src_col, (slots, 128))
        == lax.broadcasted_iota(jnp.int32, (slots, 128), 1),
        1.0,
        0.0,
    ).astype(jnp.bfloat16)
    sets = table.shape[0]
    pick_set = jnp.where(
        jnp.broadcast_to(weight_col, (slots, sets))
        == lax.broadcasted_iota(jnp.int32, (slots, sets), 1),
        1.0,
        0.0,
    ).astype(jnp.bfloat16)
    state_high, state_low = split(state[...])
    table_high, table_low = split(table[...])
    blocks = dot(pick_src, state_high, 1, 1) + dot(pick_src, state_low, 1, 1)
    scales = dot(pick_set, table_high, 1, 0) + dot(pick_set, table_low, 1, 0)
    sending = blocks * scales
    tail = jnp.concatenate(
        [sending[:, 256:320], jnp.broadcast_to(target_col, (slots, 64))], axis=1
    )
    for c, chunk in enumerate((sending[:, 0:128], sending[:, 128:256], tail)):
        for o in range(2):
            zone_out[pl.ds(o * 3 + c, ZONES, stride=8)] = chunk[o * ZONES : (o + 1) * ZONES]

    def block(row, p):
        return pl.ds(pl.multiple_of((row * NY + p) * 8, 8), BLOCK)

    def zone_send(row, p):
        pltpu.make_async_remote_copy(
            src_ref=zone_out.at[block(row, p)],
            dst_ref=zone_in.at[block(h, place)],
            send_sem=send3,
            recv_sem=recv3,
            device_id=(me, zone_at(row, p)),
            device_id_type=MESH,
        ).start()

    def span(j, there):
        start = CHIP_ROWS * j + ROWS[0] * there
        return pl.ds(pl.multiple_of(start, 8), ROWS[there])

    def first_copy(j, there):
        return pltpu.make_async_remote_copy(
            src_ref=state.at[span(j, there)],
            dst_ref=spread_in.at[me, pl.ds(0, ROWS[there])],
            send_sem=send1,
            recv_sem=recv1,
            device_id=(j * NC + there, zone),
            device_id_type=MESH,
        )

    def second_copy(j, there, here):
        return pltpu.make_async_remote_copy(
            src_ref=spread_out.at[j * NC + there, pl.ds(0, ROWS[here])],
            dst_ref=time_term.at[span(chip, here)],
            send_sem=send2,
            recv_sem=recv2,
            device_id=(j * NC + there, zone),
            device_id_type=MESH,
        )

    def whole(ref, send_sem, recv_sem):
        return pltpu.make_async_remote_copy(
            src_ref=ref,
            dst_ref=ref,
            send_sem=send_sem,
            recv_sem=recv_sem,
            device_id=(chip * NC + 1 - core, zone),
            device_id_type=MESH,
        )

    zones_whole = whole(zone_in.at[pl.ds(0, BLOCK * (ZONES - 1))], send3, recv3)

    def first_received(here):
        return whole(spread_in.at[pl.ds(0, NT - 1), pl.ds(0, ROWS[here])], send1, recv1)

    def second_received(here):
        rows = CHIP_ROWS * CHIPS - ROWS[here]
        return whole(time_term.at[pl.ds(0, rows)], send2, recv2)

    def first_sent(here):
        rows = CHIP_ROWS * CHIPS - ROWS[here]
        return whole(time_term.at[pl.ds(0, rows)], send1, recv1)

    def second_sent(here):
        return whole(spread_in.at[pl.ds(0, NT - 1), pl.ds(0, ROWS[here])], send2, recv2)

    def on_core(step):
        for here in range(NC):

            @pl.when(core == here)
            def _():
                step(here)

    def peers(low, high, step):
        def one(p):
            there = inst_at(p)
            for c in range(NC):

                @pl.when(lax.rem(there, NC) == c)
                def _():
                    step(lax.div(there, NC), c)

        each(low, high, one)

    before(zone_send)
    peers(0, inst_mine, lambda j, there: first_copy(j, there).start())

    def keep_own(here):
        spread_in[me, 0 : ROWS[here]] = state[span(chip, here)]

    on_core(keep_own)
    zone_in[block(h, place)] = zone_out[block(h, place)]
    for load in loads[6:]:
        load.wait()
    clusters = state.shape[1]
    key = kind[...] * clusters + col[...]
    cluster_ids = lax.broadcasted_iota(jnp.int32, (clusters, clusters), 0)
    total = None
    for t in range(jac.shape[0]):
        hits = None
        for j in range(key.shape[0]):
            row = jnp.broadcast_to(key[j : j + 1] - t * clusters, (clusters, clusters))
            hit = jnp.where(cluster_ids == row, 1.0, 0.0)
            hits = hit if hits is None else hits + hit
        gathered = dot(state_high, hits.astype(jnp.bfloat16), 1, 0)
        gathered_high, gathered_low = split(gathered)
        both = jnp.concatenate([gathered_high, gathered_low], axis=1)
        product = dot(jac[t], both, 1, 0)
        total = product if total is None else total + product
    total_ref[...] = source[...] + (total[:, 0:clusters] + total[:, clusters:])

    wait_for(inst_ready, NT - 1 - inst_mine)
    peers(inst_mine + 1, NT, lambda j, there: first_copy(j, there).start())

    wait_for(zone_ready.at[h], NY - 1 - place)
    each(last, h + 1, lambda row: each(place + 1, NY, lambda p: zone_send(row, p)))

    coeff = coefficients()

    def transform(here):
        first_received(here).wait_recv()
        for r in range(0, ROWS[here], 8):
            parts = [spread_in[m, r : r + 8] for m in range(NT)]
            for n in range(NT):
                value = parts[0] * coeff[n]
                for m in range(1, NT):
                    value = value + parts[m] * coeff[(n - m) % NT]
                spread_out[n, r : r + 8] = value
        send = lambda j, there: second_copy(j, there, here).start()
        peers(0, inst_mine, send)
        peers(inst_mine + 1, NT, send)
        time_term[span(chip, here)] = spread_out[me, 0 : ROWS[here]]

    on_core(transform)

    def row_send(row):
        pl.semaphore_wait(zone_ready.at[row], NY - place * far(h, row))
        each(0, NY, lambda p: zone_send(row, p))

    each(h + 1, NH, row_send)

    on_core(lambda here: second_received(here).wait_recv())
    lanes = lax.broadcasted_iota(jnp.int32, (slots, 128), 1)
    active = lax.broadcasted_iota(jnp.int32, (1, clusters), 1) < count[0]
    mask_ref[...] = jnp.where(active, 1.0, 0.0)
    total_ref[...] = total_ref[...] + time_term[...]

    zones_whole.wait_recv()
    chunks = [
        jnp.concatenate(
            [zone_in[pl.ds(o * 3 + c, ZONES, stride=8)] for o in range(2)], axis=0
        )
        for c in range(3)
    ]
    targets = jnp.where(lanes < 64, pltpu.roll(chunks[2], 64, 1), chunks[2])
    landing = jnp.where(targets == (lanes + 1).astype(jnp.float32), 1.0, 0.0).astype(
        jnp.bfloat16
    )
    for c, rows in enumerate((128, 128, 64)):
        high, low = split(chunks[c])
        iface = dot(high, landing, 0, 0) + dot(low, landing, 0, 0)
        at = pl.ds(c * 128, rows)
        combined_ref[at] = total_ref[at] - iface[0:rows]

    def drain(here):
        first_sent(here).wait_send()
        second_sent(here).wait_send()

    on_core(drain)
    zones_whole.wait_send()


def on_device(
    state,
    source,
    jac_table,
    pattern_col,
    pattern_type,
    pseudo_step,
    zone_count,
    link_src,
    link_owner,
    link_dest,
    link_weight,
    iface_table,
):
    state_t = state[0].T
    source_t = source[0].T
    width, clusters = state_t.shape
    kinds = jac_table.shape[0]
    links = link_src.shape[1]
    f32, i32, bf16 = jnp.float32, jnp.int32, jnp.bfloat16
    dma = pltpu.SemaphoreType.DMA
    regular = pltpu.SemaphoreType.REGULAR
    combined, mask = pl.pallas_call(
        kernel,
        out_shape=[
            pltpu.VMEM((width, clusters), f32),
            pltpu.VMEM((1, clusters), f32),
        ],
        in_specs=[pl.BlockSpec(memory_space=pltpu.HBM)] * 11,
        out_specs=[pl.BlockSpec(memory_space=pltpu.VMEM)] * 2,
        scratch_shapes=[
            pltpu.VMEM((width, clusters), f32),
            pltpu.VMEM((width, clusters), f32),
            pltpu.VMEM((kinds, width, width), bf16),
            pltpu.VMEM((4, clusters), i32),
            pltpu.VMEM((4, clusters), i32),
            pltpu.VMEM((1, links), i32),
            pltpu.VMEM((1, links), i32),
            pltpu.VMEM((1, links), i32),
            pltpu.VMEM((1, links), i32),
            pltpu.VMEM(iface_table.shape, f32),
            pltpu.SMEM((1,), i32),
            pltpu.VMEM((width, clusters), f32),
            pltpu.VMEM((NT, ROWS[0], clusters), f32),
            pltpu.VMEM((NT, ROWS[0], clusters), f32),
            pltpu.VMEM((width, clusters), f32),
            pltpu.VMEM((ZONES * 8, 128), f32),
            pltpu.VMEM((ZONES * 8, 128), f32),
            dma((11,)),
            dma(()),
            dma(()),
            dma(()),
            dma(()),
            dma(()),
            dma(()),
            regular(()),
            regular((NH,)),
        ],
        compiler_params=pltpu.CompilerParams(collective_id=0, has_side_effects=True),
        name="section",
    )(
        state_t,
        source_t,
        jac_table,
        pattern_col.T,
        pattern_type.T,
        link_src,
        link_owner.reshape(1, links),
        link_dest,
        link_weight,
        iface_table,
        zone_count,
    )
    residual = jnp.where(mask > 0.5, combined, 0.0)
    updated = state_t - pseudo_step * residual
    return (updated.T[None], residual.T[None])


def solution(mesh):
    placed = (
        P("inst", "zone", None),
        P("inst", "zone", None),
        P("zone", None, None),
        P("zone", None),
        P("zone", None),
        P("inst", "zone"),
        P("zone"),
        P("inst", "zone"),
        P("inst", "zone", None),
        P("inst", "zone"),
        P("inst", "zone"),
        P(),
    )
    return jax.shard_map(
        on_device,
        mesh=mesh,
        in_specs=placed,
        out_specs=(P("inst", "zone", None), P("inst", "zone", None)),
        check_vma=False,
    )
```

time: 30.8 us -> 22.5 us (0.73)
  the two profiles are of different devices: /device:TPU:1 before, /device:TPU:60 now
where the time goes in v2:
time: 22.5 us; the launch traced here: 22.4 us
  Pallas kernels  20.2 us (90%)
  between operations  1.36 us (6%)
  other arithmetic  0.75 us (3%)
    pallas_call x1, Pallas kernels, on_device(): pl.pallas_call(kernel, out_shape=[pltpu.VMEM((width, clusters), f32), plt...  20.2 us
    broadcast_in_dim x1, other arithmetic, on_device(): return (updated.T[None], residual.T[None])  0.75 us

profile of v2, /device:TPU:60, one launch (start us, length us, event | category | flops | bytes accessed | tf_op | source)
XLA Modules:
  0.0 22.4 jit_solution(6158480673079734742)
XLA Ops:
  0.6 0.0 copy-start
  0.6 0.0 copy-start.1
  1.3 20.2 %section.1 = (f32[320,128]{1,0:T(8,128)S(1)}, f32[1,128]{1,0:T(1,128)S(1)}) custom-call(f32[320,128]{1,0:T(8,128)} %bitcast.21, f32[320,128]{1,0:T(8,128)} %bitcast.22, bf16[8,320,320]{2,1,0:T(8,128)(2,1)} %jac_hbm.1, s32[4,128]{1,0:T(4,128)} %bitcast.23, s32[4,128]{1,0:T(4,128)} %bitcast.24, s32[1,32]{1,0:T(1,128)} %src_hbm.1, s32[1,32]{1,0:T(1,128)} %bitcast.25, ...), custom_call_target="tpu_custom_call" | custom-call | tf_op jit(solution)/shard_map/section/pallas_call | solution.py:423
  21.6 0.0 copy-done
  21.6 0.0 copy-done.1
  21.6 0.7 %select_bitcast_fusion = (f32[1,128,320]{1,2,0:T(8,128)}, f32[1,128,320]{1,2,0:T(8,128)}) fusion(f32[320,128]{1,0:T(8,128)S(1)} %get-tuple-element.5, pred[128]{0:T(512)(128)(4,1)S(1)} %compare_bitcast_fusion, f32[128]{0:T(128)S(1)} %bitcast.26, f32[1,128,320]{1,2,0:T(8,128)S(1)} %copy-done), kind=kLoop, calls=%fused_computation.1 | loop fusion | flops 122880 | bytes 656000 | tf_op jit(solution)/shard_map/broadcast_in_dim | solution.py:476
  (1 shorter events, 0.0 us)
Async XLA Ops:
  0.6 21.0 %copy-start = (f32[1,128,320]{1,2,0:T(8,128)S(1)}, f32[1,128,320]{1,2,0:T(8,128)}, u32[]{:S(2)}) copy-start(f32[1,128,320]{1,2,0:T(8,128)} %param.12) | copy-start | bytes 491524
  0.6 21.0 %copy-start.1 = (f32[1,128]{1,0:T(1,128)S(1)}, f32[1,128]{1,0:T(1,128)}, u32[]{:S(2)}) copy-start(f32[1,128]{1,0:T(1,128)} %param.17) | copy-start | bytes 1540

commit v3 on v2

--- a/solution.py
+++ b/solution.py
@@ -105,21 +105,34 @@
     zone = lax.axis_index("zone")
     chip, core = lax.div(me, NC), lax.rem(me, NC)
     h, y = lax.div(zone, NY), lax.rem(zone, NY)
+    def turn(j, by):
+        moved = jnp.minimum(lax.div(h, 2), jnp.minimum(lax.div(j, 2), lax.div(5, j + 1)))
+        return j + moved * (2 + lax.rem(j - 2 + NX * 3 + by, 3) - j)
+
     inst_shift = 1 - jnp.minimum(zone, 1)
-    inst_mine = lax.rem(me + NT - inst_shift, NT)
+    inst_mine = lax.rem(NC * turn(chip, 1) + core + NT - inst_shift, NT)
     place = y_place(y)
 
     def inst_at(p):
-        return lax.rem(p + inst_shift, NT)
+        i = lax.rem(p + inst_shift, NT)
+        return NC * turn(lax.div(i, NC), 2) + lax.rem(i, NC)
 
     def zone_at(row, p):
         return row * NY + y_place(p)
 
-    def far(low, high):
-        return jnp.minimum(low + NH - 1 - high, 1)
+    def one_of(row, high):
+        late = lax.div(high, 2)
+        first = 1 - jnp.minimum(row, 1)
+        return late * first, late * (1 - first) * (1 - lax.div(row, 2))
 
     def reach(row, high):
-        return NY - far(row, high) * (NY - 1 - place)
+        first, second = one_of(row, high)
+        up_to = place + 1
+        return up_to + first * (NY - up_to) + second * (jnp.maximum(up_to, 5) - up_to)
+
+    def begin(row, high):
+        first, second = one_of(row, high)
+        return place - place * (first + second * (1 - lax.div(place, 5)))
 
     def before(step):
         each(0, h, lambda row: each(0, reach(row, h), lambda p: step(row, p)))
@@ -127,7 +140,7 @@
 
     def after(step):
         each(place + 1, NY, lambda p: step(h, p))
-        each(h + 1, NH, lambda row: each(place * far(h, row), NY, lambda p: step(row, p)))
+        each(h + 1, NH, lambda row: each(begin(h, row), NY, lambda p: step(row, p)))
 
     barrier = pltpu.get_barrier_semaphore()
 
@@ -162,11 +175,6 @@
 
     each(inst_mine + 1, NT, lambda p: signal(barrier, inst_at(p), zone))
     after(lambda row, p: signal(barrier, me, zone_at(row, p)))
-
-    last = lax.div(h, NH - 1)
-    wait_for(barrier, inst_mine + (place + 1) * (h + 1) - 1 + last * (NY - 1 - place))
-    each(0, inst_mine, lambda p: signal(inst_ready, inst_at(p), zone))
-    before(lambda row, p: signal(zone_ready.at[h], me, zone_at(row, p)))
 
     for load in loads[:6]:
         load.wait()
@@ -242,6 +250,15 @@
             device_id_type=MESH,
         ).start()
 
+    earlier_zones = place
+    for row in range(NH - 1):
+        earlier_zones = earlier_zones + reach(jnp.int32(row), h) * jnp.minimum(lax.div(h, row + 1), 1)
+    wait_for(barrier, inst_mine + earlier_zones)
+    before(zone_send)
+    team = lax.div(inst_mine, 8) + lax.div(inst_mine, NT - 1)
+    each(0, inst_mine, lambda p: signal(inst_ready.at[team], inst_at(p), zone))
+    before(lambda row, p: signal(zone_ready.at[h], me, zone_at(row, p)))
+
     def span(j, there):
         start = CHIP_ROWS * j + ROWS[0] * there
         return pl.ds(pl.multiple_of(start, 8), ROWS[there])
@@ -310,7 +327,6 @@
 
         each(low, high, one)
 
-    before(zone_send)
     peers(0, inst_mine, lambda j, there: first_copy(j, there).start())
 
     def keep_own(here):
@@ -337,11 +353,13 @@
         total = product if total is None else total + product
     total_ref[...] = source[...] + (total[:, 0:clusters] + total[:, clusters:])
 
-    wait_for(inst_ready, NT - 1 - inst_mine)
-    peers(inst_mine + 1, NT, lambda j, there: first_copy(j, there).start())
+    for team_there, (low, high) in enumerate(((0, 8), (8, NT - 1), (NT - 1, NT))):
+        first = jnp.clip(inst_mine + 1, low, high)
+        wait_for(inst_ready.at[team_there], high - first)
+        peers(first, high, lambda j, there: first_copy(j, there).start())
 
     wait_for(zone_ready.at[h], NY - 1 - place)
-    each(last, h + 1, lambda row: each(place + 1, NY, lambda p: zone_send(row, p)))
+    each(0, h + 1, lambda row: each(reach(row, h), NY, lambda p: zone_send(row, p)))
 
     coeff = coefficients()
 
@@ -362,7 +380,7 @@
     on_core(transform)
 
     def row_send(row):
-        pl.semaphore_wait(zone_ready.at[row], NY - place * far(h, row))
+        pl.semaphore_wait(zone_ready.at[row], NY - begin(h, row))
         each(0, NY, lambda p: zone_send(row, p))
 
     each(h + 1, NH, row_send)
@@ -453,7 +471,7 @@
             dma(()),
             dma(()),
             dma(()),
-            regular(()),
+            regular((3,)),
             regular((NH,)),
         ],
         compiler_params=pltpu.CompilerParams(collective_id=0, has_side_effects=True),

time: 22.5 us -> 21.1 us (0.938)
  the two profiles are of different devices: /device:TPU:60 before, /device:TPU:6 now
where the time goes in v3:
time: 21.1 us; the launch traced here: 20.9 us
  Pallas kernels  18.8 us (89%)
  between operations  1.36 us (6%)
  other arithmetic  0.75 us (4%)
    pallas_call x1, Pallas kernels, on_device(): pl.pallas_call(kernel, out_shape=[pltpu.VMEM((width, clusters), f32), plt...  18.8 us
    broadcast_in_dim x1, other arithmetic, on_device(): return (updated.T[None], residual.T[None])  0.75 us

profile of v3, /device:TPU:6, one launch (start us, length us, event | category | flops | bytes accessed | tf_op | source)
XLA Modules:
  0.0 20.9 jit_solution(16693578501806642085)
XLA Ops:
  0.6 0.0 copy-start
  0.6 0.0 copy-start.1
  1.3 18.8 %section.1 = (f32[320,128]{1,0:T(8,128)S(1)}, f32[1,128]{1,0:T(1,128)S(1)}) custom-call(f32[320,128]{1,0:T(8,128)} %bitcast.21, f32[320,128]{1,0:T(8,128)} %bitcast.22, bf16[8,320,320]{2,1,0:T(8,128)(2,1)} %jac_hbm.1, s32[4,128]{1,0:T(4,128)} %bitcast.23, s32[4,128]{1,0:T(4,128)} %bitcast.24, s32[1,32]{1,0:T(1,128)} %src_hbm.1, s32[1,32]{1,0:T(1,128)} %bitcast.25, ...), custom_call_target="tpu_custom_call" | custom-call | tf_op jit(solution)/shard_map/section/pallas_call | solution.py:441
  20.2 0.0 copy-done
  20.2 0.0 copy-done.1
  20.2 0.7 %select_bitcast_fusion = (f32[1,128,320]{1,2,0:T(8,128)}, f32[1,128,320]{1,2,0:T(8,128)}) fusion(f32[320,128]{1,0:T(8,128)S(1)} %get-tuple-element.5, pred[128]{0:T(512)(128)(4,1)S(1)} %compare_bitcast_fusion, f32[128]{0:T(128)S(1)} %bitcast.26, f32[1,128,320]{1,2,0:T(8,128)S(1)} %copy-done), kind=kLoop, calls=%fused_computation.1 | loop fusion | flops 122880 | bytes 656000 | tf_op jit(solution)/shard_map/broadcast_in_dim | solution.py:494
  (1 shorter events, 0.0 us)
Async XLA Ops:
  0.6 19.5 %copy-start = (f32[1,128,320]{1,2,0:T(8,128)S(1)}, f32[1,128,320]{1,2,0:T(8,128)}, u32[]{:S(2)}) copy-start(f32[1,128,320]{1,2,0:T(8,128)} %param.12) | copy-start | bytes 491524
  0.6 19.5 %copy-start.1 = (f32[1,128]{1,0:T(1,128)S(1)}, f32[1,128]{1,0:T(1,128)}, u32[]{:S(2)}) copy-start(f32[1,128]{1,0:T(1,128)} %param.17) | copy-start | bytes 1540

commit v4 on v3

--- a/solution.py
+++ b/solution.py
@@ -128,15 +128,11 @@
     def reach(row, high):
         first, second = one_of(row, high)
         up_to = place + 1
-        return up_to + first * (NY - up_to) + second * (jnp.maximum(up_to, 5) - up_to)
+        return up_to + first * (NY - up_to) + second * (jnp.maximum(up_to, 6) - up_to)
 
     def begin(row, high):
         first, second = one_of(row, high)
-        return place - place * (first + second * (1 - lax.div(place, 5)))
-
-    def before(step):
-        each(0, h, lambda row: each(0, reach(row, h), lambda p: step(row, p)))
-        each(0, place, lambda p: step(h, p))
+        return place - place * (first + second * (1 - lax.div(place, 6)))
 
     def after(step):
         each(place + 1, NY, lambda p: step(h, p))
@@ -254,10 +250,16 @@
     for row in range(NH - 1):
         earlier_zones = earlier_zones + reach(jnp.int32(row), h) * jnp.minimum(lax.div(h, row + 1), 1)
     wait_for(barrier, inst_mine + earlier_zones)
-    before(zone_send)
+
+    def hello(row, p):
+        zone_send(row, p)
+        signal(zone_ready.at[h], me, zone_at(row, p))
+
+    each(0, jnp.minimum(h, 1), lambda row: each(0, reach(row, h), lambda p: hello(row, p)))
     team = lax.div(inst_mine, 8) + lax.div(inst_mine, NT - 1)
     each(0, inst_mine, lambda p: signal(inst_ready.at[team], inst_at(p), zone))
-    before(lambda row, p: signal(zone_ready.at[h], me, zone_at(row, p)))
+    each(1, h, lambda row: each(0, reach(row, h), lambda p: hello(row, p)))
+    each(0, place, lambda p: hello(h, p))
 
     def span(j, there):
         start = CHIP_ROWS * j + ROWS[0] * there
@@ -402,9 +404,9 @@
     landing = jnp.where(targets == (lanes + 1).astype(jnp.float32), 1.0, 0.0).astype(
         jnp.bfloat16
     )
+    landing = jnp.concatenate([landing, landing], axis=0)
     for c, rows in enumerate((128, 128, 64)):
-        high, low = split(chunks[c])
-        iface = dot(high, landing, 0, 0) + dot(low, landing, 0, 0)
+        iface = dot(jnp.concatenate(split(chunks[c]), axis=0), landing, 0, 0)
         at = pl.ds(c * 128, rows)
         combined_ref[at] = total_ref[at] - iface[0:rows]
 

time: 21.1 us -> 21 us (level)
  no operation moved by 1% of the time
where the time goes in v4:
time: 21 us; the launch traced here: 20.9 us
  Pallas kernels  18.8 us (90%)
  between operations  1.36 us (6%)
  other arithmetic  0.75 us (4%)
    pallas_call x1, Pallas kernels, on_device(): pl.pallas_call(kernel, out_shape=[pltpu.VMEM((width, clusters), f32), plt...  18.8 us
    broadcast_in_dim x1, other arithmetic, on_device(): return (updated.T[None], residual.T[None])  0.75 us

profile of v4, /device:TPU:6, one launch (start us, length us, event | category | flops | bytes accessed | tf_op | source)
XLA Modules:
  0.0 20.9 jit_solution(9424539887937743862)
XLA Ops:
  0.6 0.0 copy-start
  0.6 0.0 copy-start.1
  1.3 18.8 %section.1 = (f32[320,128]{1,0:T(8,128)S(1)}, f32[1,128]{1,0:T(1,128)S(1)}) custom-call(f32[320,128]{1,0:T(8,128)} %bitcast.21, f32[320,128]{1,0:T(8,128)} %bitcast.22, bf16[8,320,320]{2,1,0:T(8,128)(2,1)} %jac_hbm.1, s32[4,128]{1,0:T(4,128)} %bitcast.23, s32[4,128]{1,0:T(4,128)} %bitcast.24, s32[1,32]{1,0:T(1,128)} %src_hbm.1, s32[1,32]{1,0:T(1,128)} %bitcast.25, ...), custom_call_target="tpu_custom_call" | custom-call | tf_op jit(solution)/shard_map/section/pallas_call | solution.py:443
  20.1 0.0 copy-done
  20.1 0.0 copy-done.1
  20.2 0.7 %select_bitcast_fusion = (f32[1,128,320]{1,2,0:T(8,128)}, f32[1,128,320]{1,2,0:T(8,128)}) fusion(f32[320,128]{1,0:T(8,128)S(1)} %get-tuple-element.5, pred[128]{0:T(512)(128)(4,1)S(1)} %compare_bitcast_fusion, f32[128]{0:T(128)S(1)} %bitcast.26, f32[1,128,320]{1,2,0:T(8,128)S(1)} %copy-done), kind=kLoop, calls=%fused_computation.1 | loop fusion | flops 122880 | bytes 656000 | tf_op jit(solution)/shard_map/broadcast_in_dim | solution.py:496
  (1 shorter events, 0.0 us)
Async XLA Ops:
  0.6 19.5 %copy-start = (f32[1,128,320]{1,2,0:T(8,128)S(1)}, f32[1,128,320]{1,2,0:T(8,128)}, u32[]{:S(2)}) copy-start(f32[1,128,320]{1,2,0:T(8,128)} %param.12) | copy-start | bytes 491524
  0.6 19.5 %copy-start.1 = (f32[1,128]{1,0:T(1,128)S(1)}, f32[1,128]{1,0:T(1,128)}, u32[]{:S(2)}) copy-start(f32[1,128]{1,0:T(1,128)} %param.17) | copy-start | bytes 1540

commit v5 on v4

--- a/solution.py
+++ b/solution.py
@@ -464,8 +464,8 @@
             pltpu.VMEM((NT, ROWS[0], clusters), f32),
             pltpu.VMEM((NT, ROWS[0], clusters), f32),
             pltpu.VMEM((width, clusters), f32),
-            pltpu.VMEM((ZONES * 8, 128), f32),
-            pltpu.VMEM((ZONES * 8, 128), f32),
+            pltpu.VMEM((ZONES * 8 + 8, 128), f32),
+            pltpu.VMEM((ZONES * 8 + 8, 128), f32),
             dma((11,)),
             dma(()),
             dma(()),

time: 21 us -> 21 us (level)
  no operation moved by 1% of the time
where the time goes in v5:
time: 21 us; the launch traced here: 20.9 us
  Pallas kernels  18.8 us (90%)
  between operations  1.36 us (6%)
  other arithmetic  0.75 us (4%)
    pallas_call x1, Pallas kernels, on_device(): pl.pallas_call(kernel, out_shape=[pltpu.VMEM((width, clusters), f32), plt...  18.8 us
    broadcast_in_dim x1, other arithmetic, on_device(): return (updated.T[None], residual.T[None])  0.75 us

profile of v5, /device:TPU:6, one launch (start us, length us, event | category | flops | bytes accessed | tf_op | source)
XLA Modules:
  0.0 20.9 jit_solution(11874313128744402447)
XLA Ops:
  0.6 0.0 copy-start
  0.6 0.0 copy-start.1
  1.3 18.8 %section.1 = (f32[320,128]{1,0:T(8,128)S(1)}, f32[1,128]{1,0:T(1,128)S(1)}) custom-call(f32[320,128]{1,0:T(8,128)} %bitcast.21, f32[320,128]{1,0:T(8,128)} %bitcast.22, bf16[8,320,320]{2,1,0:T(8,128)(2,1)} %jac_hbm.1, s32[4,128]{1,0:T(4,128)} %bitcast.23, s32[4,128]{1,0:T(4,128)} %bitcast.24, s32[1,32]{1,0:T(1,128)} %src_hbm.1, s32[1,32]{1,0:T(1,128)} %bitcast.25, ...), custom_call_target="tpu_custom_call" | custom-call | tf_op jit(solution)/shard_map/section/pallas_call | solution.py:443
  20.1 0.0 copy-done
  20.1 0.0 copy-done.1
  20.2 0.7 %select_bitcast_fusion = (f32[1,128,320]{1,2,0:T(8,128)}, f32[1,128,320]{1,2,0:T(8,128)}) fusion(f32[320,128]{1,0:T(8,128)S(1)} %get-tuple-element.5, pred[128]{0:T(512)(128)(4,1)S(1)} %compare_bitcast_fusion, f32[128]{0:T(128)S(1)} %bitcast.26, f32[1,128,320]{1,2,0:T(8,128)S(1)} %copy-done), kind=kLoop, calls=%fused_computation.1 | loop fusion | flops 122880 | bytes 656000 | tf_op jit(solution)/shard_map/broadcast_in_dim | solution.py:496
  (1 shorter events, 0.0 us)
Async XLA Ops:
  0.6 19.5 %copy-start = (f32[1,128,320]{1,2,0:T(8,128)S(1)}, f32[1,128,320]{1,2,0:T(8,128)}, u32[]{:S(2)}) copy-start(f32[1,128,320]{1,2,0:T(8,128)} %param.12) | copy-start | bytes 491524
  0.6 19.5 %copy-start.1 = (f32[1,128]{1,0:T(1,128)S(1)}, f32[1,128]{1,0:T(1,128)}, u32[]{:S(2)}) copy-start(f32[1,128]{1,0:T(1,128)} %param.17) | copy-start | bytes 1540
